TPU v7x, 128 devices: a whole 4x4x4 slice. The times are simulated.
128 devices in a mesh: row: 8 (over z, core), col: 16 (over x, y).
Axes of the slice: x: 4, y: 4, z: 4, core: 2. Of those that a mesh axis runs over, the one named last changes fastest.
Arguments:
- normed: bfloat16 [8192, 7168], P(None, 'col'), may hold values from -44 to 44
- projection_weight: bfloat16 [7168, 3, 7168], P('col', None, 'row')
- adapter_down_weight: bfloat16 [7168, 16, 32], P(None, 'col'), may hold values from -0.0625 to 0.0625
- adapter_up_weight: bfloat16 [16, 2, 16, 7168], P(None, None, None, 'row'), may hold values from -0.47851562 to 0.47851562
- packed_prompt_length: int32 [64], replicated, may hold values from 64 to 512, as said below
- prompt_adapter_ids: int32 [64], replicated, may hold values from 0 to 63, as said below
- slot_adapter_ids: int32 [16], replicated, may hold values from 0 to 63, as said below
- prompt_page_slots: int32 [64, 4], replicated, may hold values from -1 to 159, as said below
Outputs:
- attended: bfloat16 [8192, 7168], P('col', 'row')
- kv_cache: bfloat16 [160, 128, 2, 7168], P('col', None, None, 'row')
Inputs may be any that keep to these rules, and one draw needn't show every extreme that they name: `packed_prompt_length`: the 64 lengths sum to 8192; one of them is exactly 512 and one exactly 64. `slot_adapter_ids`: distinct adapter ids. `prompt_adapter_ids`: every entry is one of slot_adapter_ids, and every loaded adapter is named by at least one prompt. `prompt_page_slots`: entry [i, j] is -1 where 128 * j >= packed_prompt_length[i]; otherwise it lies among slots 10 * c to 10 * c + 9, where c is the block of 512 packed tokens that holds the page's last token. No slot is named twice.
All inputs are finite; a program needn't handle non-finite values.
Results may differ from a plain program's by a relative error of at most 0.0072.
Values may be sent and summed in bfloat16 or wider, within the bound.
A program may use at most 256 MiB of HBM per device.

v0:
```python
import jax
import jax.numpy as jnp
from jax import lax
from jax.sharding import PartitionSpec as P

HEAD_DIM = 128
PAGE = 128
NEAR = 1
SLOTS_DEV = 10
adapter_scale = 2.0
masked_score = -1e30


def shifted(block, axis, distance):
    devices = range(lax.axis_size(axis))
    route = [(i - distance, i) for i in devices if i - distance in devices]
    return lax.ppermute(block, axis, route)


def start_table(packed_prompt_length):
    prompt_ends = jnp.cumsum(packed_prompt_length)
    return prompt_ends - packed_prompt_length


def slot_table(prompt_adapter_ids, slot_adapter_ids):
    active_slots = slot_adapter_ids.shape[0]
    matched = slot_adapter_ids[None, :] == prompt_adapter_ids[:, None]
    return jnp.sum(
        jnp.where(matched, jnp.arange(active_slots, dtype=jnp.int32)[None, :], 0), axis=1
    )


def token_prompts(positions, prompt_starts):
    inside = (positions[:, None] >= prompt_starts[None, :]).astype(jnp.int32)
    return jnp.sum(inside, axis=1) - 1


def token_slots(prompts, slot_of):
    prompt_count = slot_of.shape[0]
    onehot = prompts[:, None] == jnp.arange(prompt_count, dtype=jnp.int32)[None, :]
    return jnp.sum(jnp.where(onehot, slot_of[None, :], 0), axis=1)


def down_term(row_block, slots_here, down_cols, active_slots):
    combined_output = jnp.dot(row_block, down_cols, preferred_element_type=jnp.float32)
    combined_output = combined_output.reshape(row_block.shape[0], active_slots, -1)
    pick_slot = slots_here[:, None] == jnp.arange(active_slots, dtype=jnp.int32)[None, :]
    return jnp.sum(jnp.where(pick_slot[:, :, None], combined_output, 0.0), axis=1)


def local(
    normed,
    projection_weight,
    adapter_down_weight,
    adapter_up_weight,
    packed_prompt_length,
    prompt_adapter_ids,
    slot_adapter_ids,
    prompt_page_slots,
):
    col_count = lax.axis_size("col")
    row_count = lax.axis_size("row")
    col_index = lax.axis_index("col")
    my_row = lax.axis_index("row")
    tok_all, width_loc = normed.shape
    tok_blk = tok_all // col_count
    head_column_span = projection_weight.shape[2]
    heads_loc = head_column_span // HEAD_DIM
    active_slots = slot_adapter_ids.shape[0]
    adapter_rank_width = adapter_up_weight.shape[2]
    prompt_starts = start_table(packed_prompt_length)
    slot_of = slot_table(prompt_adapter_ids, slot_adapter_ids)
    block_start = col_index * tok_blk
    mine = block_start + jnp.arange(tok_blk, dtype=jnp.int32)
    mine_prompts = token_prompts(mine, prompt_starts)
    mine_slots = token_slots(mine_prompts, slot_of)
    down_weight_slices = lax.all_to_all(
        adapter_down_weight, "col", split_axis=0, concat_axis=1, tiled=True
    )
    down_cols = down_weight_slices.reshape(width_loc, -1)
    own_rows = lax.all_to_all(normed, "col", split_axis=0, concat_axis=1, tiled=True)
    weight_piece = lax.all_gather(projection_weight, "col", axis=0, tiled=True)
    flat_piece = weight_piece.reshape(weight_piece.shape[0], -1)
    projection_total = jnp.dot(own_rows, flat_piece, preferred_element_type=jnp.float32)
    rows_per = tok_all // row_count
    row_first = my_row * rows_per
    row_positions = row_first + jnp.arange(rows_per, dtype=jnp.int32)
    row_slots = token_slots(token_prompts(row_positions, prompt_starts), slot_of)
    row_part = lax.dynamic_slice_in_dim(normed, row_first, rows_per, 0)
    summed = lax.psum(down_term(row_part, row_slots, down_cols, active_slots), "col")
    down_every = lax.all_gather(summed.astype(jnp.bfloat16), "row", axis=0, tiled=True)
    local_down_output = lax.dynamic_slice_in_dim(down_every, block_start, tok_blk, 0)
    pick_half = (mine_slots[:, None] == jnp.arange(active_slots, dtype=jnp.int32)[None, :]).astype(
        jnp.bfloat16
    )

    def reduced_rank_rows(low_part, slot_membership):
        token_spread = (pick_half[:, :, None] * low_part[:, None, :]).reshape(
            tok_blk, active_slots * adapter_rank_width
        )
        up_weight_table = adapter_up_weight[:, slot_membership].reshape(
            active_slots * adapter_rank_width, head_column_span
        )
        return jnp.dot(token_spread, up_weight_table, preferred_element_type=jnp.float32)

    query_token_rows = (
        projection_total[:, :head_column_span]
        + adapter_scale * reduced_rank_rows(local_down_output[:, :adapter_rank_width], 0)
    ).astype(jnp.bfloat16)
    key_rows = projection_total[:, head_column_span : 2 * head_column_span].astype(jnp.bfloat16)
    value_token_rows = (
        projection_total[:, 2 * head_column_span :]
        + adapter_scale * reduced_rank_rows(local_down_output[:, adapter_rank_width:], 1)
    ).astype(jnp.bfloat16)
    own_kv = jnp.stack([key_rows, value_token_rows], axis=1)
    earlier = [shifted(own_kv, "col", 1)]
    window = jnp.concatenate(earlier[::-1] + [own_kv], axis=0)
    window_len = window.shape[0]
    window_pos = block_start - NEAR * tok_blk + jnp.arange(window_len, dtype=jnp.int32)
    window_prompts = token_prompts(window_pos, prompt_starts)
    allowed = (mine_prompts[:, None] == window_prompts[None, :]) & (
        window_pos[None, :] <= mine[:, None]
    )
    query_heads = query_token_rows.reshape(tok_blk, heads_loc, HEAD_DIM)
    key_heads = window[:, 0].reshape(window_len, heads_loc, HEAD_DIM)
    value_heads = window[:, 1].reshape(window_len, heads_loc, HEAD_DIM)
    score_scale = HEAD_DIM ** (-0.5)
    scores = (
        jnp.einsum("qhd,khd->hqk", query_heads, key_heads, preferred_element_type=jnp.float32)
        * score_scale
    )
    limited = jnp.where(allowed[None], scores, masked_score)
    peak_score = jnp.max(limited, axis=2, keepdims=True)
    weight = jnp.where(allowed[None], jnp.exp(scores - peak_score), 0.0)
    denominator = jnp.sum(weight, axis=2)
    mixed_heads = jnp.einsum(
        "hqk,khd->qhd", weight.astype(jnp.bfloat16), value_heads, preferred_element_type=jnp.float32
    )
    attended = (
        (mixed_heads / jnp.transpose(denominator)[:, :, None])
        .reshape(tok_blk, head_column_span)
        .astype(jnp.bfloat16)
    )
    prev_kv = earlier[0]
    page_window = jnp.concatenate(
        [prev_kv, own_kv, jnp.zeros((PAGE, 2, head_column_span), jnp.bfloat16)], axis=0
    )
    max_pages = prompt_page_slots.shape[1]
    lens_rep = jnp.repeat(packed_prompt_length, max_pages)
    starts_rep = jnp.repeat(prompt_starts, max_pages)
    page_index = jnp.tile(jnp.arange(max_pages, dtype=jnp.int32), packed_prompt_length.shape[0])
    page_rows = jnp.clip(lens_rep - PAGE * page_index, 0, PAGE)
    page_first = starts_rep + PAGE * page_index
    my_slots = col_index * SLOTS_DEV + jnp.arange(SLOTS_DEV, dtype=jnp.int32)
    slot_hit = prompt_page_slots.reshape(-1)[None, :] == my_slots[:, None]
    rows_used = jnp.sum(jnp.where(slot_hit, page_rows[None, :], 0), axis=1)
    first_used = jnp.sum(jnp.where(slot_hit, page_first[None, :], 0), axis=1)
    offset = jnp.clip(first_used - (col_index - 1) * tok_blk, 0, 2 * tok_blk)
    page_lines = jnp.arange(PAGE, dtype=jnp.int32)
    pick_rows = (offset[:, None] + page_lines[None, :]).reshape(-1)
    taken_rows = jnp.take(page_window, pick_rows, axis=0).reshape(
        SLOTS_DEV, PAGE, 2, head_column_span
    )
    live_rows = (page_lines[None, :] < rows_used[:, None])[:, :, None, None]
    kv_pages = jnp.where(live_rows, taken_rows, jnp.zeros_like(taken_rows))
    return (attended, kv_pages)


def solution(mesh):
    placed = (
        P(None, "col"),
        P("col", None, "row"),
        P(None, "col", None),
        P(None, None, None, "row"),
        P(),
        P(),
        P(),
        P(),
    )
    return jax.shard_map(
        local,
        mesh=mesh,
        in_specs=placed,
        out_specs=(P("col", "row"), P("col", None, None, "row")),
        check_vma=False,
    )
```

profile of v0, /device:TPU:6, one launch (start us, length us, event | category | flops | bytes accessed | tf_op | source)
XLA Modules:
  0.0 544.9 jit_solution(5829252045479823222)
XLA Ops:
  7.2 0.0 all-gather.2.cloned.1.call-start
  7.2 0.7 all-gather.2.cloned.1.call-update
  7.9 0.5 broadcast.227
  8.4 1.9 reduce.3
  10.3 0.9 copy.105
  11.3 2.4 reshape.319
  13.7 7.4 %all-to-all-start.1 = ((bf16[16,2,7168]{2,1,0:T(2,128)(2,1)}), bf16[16,2,7168]{2,1,0:T(2,128)(2,1)S(1)}, u32[]{:S(2)}, u32[]{:S(2)}) async-start(bf16[16,2,7168]{2,1,0:T(2,128)(2,1)} %reshape.319), calls=%async_computation.1 | async-start | bytes 917504 | tf_op jit(solution)/shard_map/all_to_all | solution.py:77
  21.1 8.1 %copy.104 = bf16[56,16,8,512]{3,2,0,1:T(8,128)(2,1)} copy(bf16[56,16,8,512]{3,2,1,0:T(8,128)(2,1)} %bitcast.61) | data formatting | bytes 14680064 | tf_op jit(solution)/shard_map/all_to_all | solution.py:81
  29.2 1.7 all-to-all-done.1
  31.0 5.9 %all-to-all-start = ((bf16[16,512,448]{1,2,0:T(8,128)(2,1)}), bf16[16,512,448]{1,2,0:T(8,128)(2,1)}, u32[]{:S(2)}, u32[]{:S(2)}) async-start(bf16[16,512,448]{1,2,0:T(8,128)(2,1)} %bitcast.59), calls=%async_computation | async-start | bytes 14680064 | tf_op jit(solution)/shard_map/all_to_all | solution.py:81
  36.9 0.0 copy-done.5
  36.9 0.1 copy.82
  37.0 0.1 reduce-window.9
  37.1 0.1 reduce
  37.3 0.0 copy-done.7
  37.3 0.0 copy-done.8
  37.3 0.1 select_reduce_fusion.4
  37.4 0.1 convert_reduce_fusion.2
  37.5 0.1 select_reduce_fusion.3
  37.6 0.1 convert_reduce_fusion
  37.7 0.1 select_reduce_fusion.2
  37.9 0.1 fusion.21
  38.0 0.1 subtract_clamp_fusion
  38.1 0.1 fusion.36
  38.1 4.2 reshape.320
  42.4 7.0 %copy.84 = bf16[7168,1,32]{0,2,1:T(8,128)(2,1)S(1)} copy(bf16[7168,1,32]{2,1,0:T(2,128)(2,1)} %reshape.320) | data formatting | bytes 917504 | tf_op jit(solution)/shard_map/all_to_all | solution.py:77
  49.4 0.6 all_to_all.30
  50.0 1.9 select_reduce_fusion.1
  52.0 199.3 %all-reduce.1 = bf16[1024,32]{0,1:T(8,128)(2,1)S(1)} all-reduce(f32[1024,32]{0,1:T(8,128)S(1)} %select_reduce_fusion.1), channel_id=1, replica_groups=mesh['row'=8,'col'=16] {'col'}, use_global_device_ids=true, to_apply=%region_7.8 | all-reduce | flops 32768 | bytes 196608 | tf_op jit(solution)/shard_map/psum | solution.py:90
  251.3 13.7 %all_gather.7 = bf16[8192,32]{0,1:T(8,128)(2,1)S(1)} all-gather(bf16[1024,32]{0,1:T(8,128)(2,1)S(1)} %all-reduce.1), channel_id=1, replica_groups=mesh['row'=8,'col'=16] {'row'}, dimensions={0}, use_global_device_ids=true | all-gather | bytes 589824 | tf_op jit(solution)/shard_map/all_gather | solution.py:91
  265.0 66.0 %all-gather.2.cloned.1.call-done = bf16[7168,3,896]{2,0,1:T(8,128)(2,1)} async-done(((bf16[448,3,896]{2,0,1:T(8,128)(2,1)}), bf16[7168,3,896]{2,0,1:T(8,128)(2,1)}) %all-gather.2.cloned.1.call-update) | async-done | bytes 38535184 | tf_op jit(solution)/shard_map/all_gather | solution.py:82
  331.0 51.4 %copy.81 = bf16[7168,3,896]{0,2,1:T(8,128)(2,1)} copy(bf16[7168,3,896]{2,0,1:T(8,128)(2,1)} %all-gather.2.cloned.1.call-done) | data formatting | bytes 77070336 | tf_op jit(solution)/shard_map/all_gather | solution.py:82
  382.4 0.0 all-to-all-done
  382.4 28.4 %fusion.38 = f32[512,2688]{1,0:T(8,128)} fusion(bf16[512,7168]{0,1:T(8,128)(2,1)} %bitcast.1, bf16[7168,2688]{0,1:T(8,128)(2,1)} %bitcast.58), kind=kOutput, calls=%fused_computation.78 | convolution fusion | flops 19730006016 | bytes 51380224 | tf_op jit(solution)/shard_map/dot_general | solution.py:84
  410.8 1.6 fusion.16
  412.4 2.0 fusion.15
  414.3 1.4 pad_maximum_fusion
  415.8 1.9 collective-permute-start
  417.7 0.1 copy.91
  417.8 0.1 eq.123
  417.9 0.1 add.145
  418.0 0.1 min.20
  418.1 0.2 fusion.24
  418.3 0.1 fusion.25
  418.5 0.1 fusion.28
  418.5 0.1 iota_compare_fusion.4
  418.6 1.3 compare_and_fusion
  419.9 2.0 fusion.10
  421.9 1.5 copy.87
  423.4 41.3 %collective-permute-done = bf16[512,2,896]{2,0,1:T(8,128)(2,1)} collective-permute-done((bf16[512,2,896]{2,0,1:T(8,128)(2,1)}, bf16[512,2,896]{2,0,1:T(8,128)(2,1)}, u32[]{:S(2)}, u32[]{:S(2)}) %collective-permute-start) | collective-permute-done | bytes 1835040 | tf_op jit(solution)/shard_map/ppermute | solution.py:17
  464.7 1.8 maximum_maximum_fusion.1
  466.5 2.1 fusion.35
  468.6 3.8 copy.88
  472.5 3.1 maximum_maximum_fusion
  475.6 0.0 copy-start.3
  475.7 15.3 %copy.92 = bf16[1152,2,896]{2,1,0:T(2,128)(2,1)} copy(bf16[1152,2,896]{2,0,1:T(8,128)(2,1)S(1)} %maximum_maximum_fusion) | data formatting | bytes 8257536 | tf_op jit(solution)/shard_map/concatenate | solution.py:145
  490.9 0.0 copy-done
  490.9 2.4 copy.86
  493.3 0.0 copy-done.4
  493.3 12.7 %fusion.37 = (f32[7,512]{1,0:T(8,128)S(1)}, bf16[7,512,1024]{2,1,0:T(8,128)(2,1)}) fusion(pred[512,1024]{1,0:T(8,128)(4,1)S(1)} %copy-done.4, bf16[512,7,128]{0,2,1:T(8,128)(2,1)S(1)} %bitcast.68, bf16[1024,7,128]{0,2,1:T(8,128)(2,1)} %bitcast.62), kind=kOutput, calls=%fused_computation.77 | convolution fusion | flops 1904739328 | bytes 10631168 | tf_op jit(solution)/shard_map/sub | solution.py:134
  506.0 5.7 %fusion.12 = bf16[512,7,128]{0,2,1:T(8,128)(2,1)S(1)} fusion(bf16[1024,7,128]{0,2,1:T(8,128)(2,1)S(1)} %bitcast.63, bf16[7,512,1024]{2,1,0:T(8,128)(2,1)} %get-tuple-element.29, f32[512,7]{0,1:T(8,128)S(1)} %bitcast.72), kind=kOutput, calls=%fused_computation.25 | convolution fusion | flops 940441600 | bytes 10106880 | tf_op jit(solution)/shard_map/hqk,khd->qhd/dot_general | solution.py:136
  511.7 1.3 copy.93
  513.0 16.6 %gather_fusion = bf16[1280,2,896]{2,1,0:T(2,128)(2,1)} fusion(bf16[1152,2,896]{2,1,0:T(2,128)(2,1)} %copy.92, s32[2048]{0:T(1024)S(1)} %pad_clamp_fusion), kind=kCustom, calls=%fused_computation | custom fusion | bytes 9180160 | tf_op jit(solution)/shard_map/jit(_take)/gather | solution.py:161
  529.6 8.5 %broadcast_select_fusion.1 = bf16[10,128,2,896]{3,2,1,0:T(2,128)(2,1)} fusion(pred[10,128]{1,0:T(8,128)(4,1)S(1)} %iota_compare_fusion.4, bf16[10,128,2,896]{3,2,1,0:T(2,128)(2,1)} %bitcast.60, pred[10,128]{1,0:T(8,128)(4,1)S(1)} %fusion.28), kind=kLoop, calls=%fused_computation.7 | loop fusion | flops 4587520 | bytes 9177600 | tf_op jit(solution)/shard_map/jit(_where)/select_n | solution.py:165
  (28 shorter events, 0.2 us)
Async XLA Ops:
  7.2 323.8 %all-gather.2.cloned.1.call-start = ((), (), s32[]{:S(2)}) async-start(), calls=%async_computation.2 | async-start | bytes 40943616 | tf_op jit(solution)/shard_map/all_gather | solution.py:82
  13.7 17.3 %all-to-all-start.1 = ((bf16[16,2,7168]{2,1,0:T(2,128)(2,1)}), bf16[16,2,7168]{2,1,0:T(2,128)(2,1)S(1)}, u32[]{:S(2)}, u32[]{:S(2)}) async-start(bf16[16,2,7168]{2,1,0:T(2,128)(2,1)} %reshape.319), calls=%async_computation.1 | async-start | bytes 917504 | tf_op jit(solution)/shard_map/all_to_all | solution.py:77
  31.0 5.9 %copy-start.5 = (s32[64]{0:T(128)S(1)}, s32[64]{0:T(128)}, u32[]{:S(2)}) copy-start(s32[64]{0:T(128)} %param.12) | copy-start | bytes 772
  31.0 6.3 %copy-start.7 = (s32[64]{0:T(128)S(1)}, s32[64]{0:T(128)}, u32[]{:S(2)}) copy-start(s32[64]{0:T(128)} %param.13) | copy-start | bytes 772
  31.0 6.3 %copy-start.8 = (s32[16]{0:T(128)S(1)}, s32[16]{0:T(128)}, u32[]{:S(2)}) copy-start(s32[16]{0:T(128)} %param.14) | copy-start | bytes 196
  31.0 7.1 %copy-start.2 = (bf16[16,2,16,896]{3,2,1,0:T(8,128)(2,1)S(1)}, bf16[16,2,16,896]{3,2,1,0:T(8,128)(2,1)}, u32[]{:S(2)}) copy-start(bf16[16,2,16,896]{3,2,1,0:T(8,128)(2,1)} %param.11) | copy-start | bytes 2752516
  31.0 351.4 %all-to-all-start = ((bf16[16,512,448]{1,2,0:T(8,128)(2,1)}), bf16[16,512,448]{1,2,0:T(8,128)(2,1)}, u32[]{:S(2)}, u32[]{:S(2)}) async-start(bf16[16,512,448]{1,2,0:T(8,128)(2,1)} %bitcast.59), calls=%async_computation | async-start | bytes 14680064 | tf_op jit(solution)/shard_map/all_to_all | solution.py:81
  410.8 6.9 %copy-start.6 = (s32[64,4]{0,1:T(4,128)S(1)}, s32[64,4]{0,1:T(4,128)}, u32[]{:S(2)}) copy-start(s32[64,4]{0,1:T(4,128)} %param.15) | copy-start | bytes 3076
  415.8 49.0 %collective-permute-start = (bf16[512,2,896]{2,0,1:T(8,128)(2,1)}, bf16[512,2,896]{2,0,1:T(8,128)(2,1)}, u32[]{:S(2)}, u32[]{:S(2)}) collective-permute-start(bf16[512,2,896]{2,0,1:T(8,128)(2,1)} %pad_maximum_fusion), channel_id=1, source_target_pairs={{0,1},{1,2},{2,3},{3,4},{4,5},{5,6},{6,7},{7,8},{8,9},{9,10},{10,1... | collective-permute-start | bytes 5505032 | tf_op jit(solution)/shard_map/ppermute | solution.py:17
  475.6 15.3 %copy-start = (bf16[1024,1,896]{2,0,1:T(8,128)(2,1)S(1)}, bf16[1024,1,896]{2,0,1:T(8,128)(2,1)}, u32[]{:S(2)}) copy-start(bf16[1024,1,896]{2,0,1:T(8,128)(2,1)} %get-tuple-element.21) | copy-start | bytes 5505028
  475.6 17.7 %copy-start.3 = (bf16[512,896]{0,1:T(8,128)(2,1)S(1)}, bf16[512,896]{0,1:T(8,128)(2,1)}, u32[]{:S(2)}) copy-start(bf16[512,896]{0,1:T(8,128)(2,1)} %copy.87) | copy-start | bytes 2752516
  475.6 17.7 %copy-start.4 = (pred[512,1024]{1,0:T(8,128)(4,1)S(1)}, pred[512,1024]{1,0:T(8,128)(4,1)}, u32[]{:S(2)}) copy-start(pred[512,1024]{1,0:T(8,128)(4,1)} %compare_and_fusion) | copy-start | bytes 1572868
  493.3 12.7 %copy-start.1 = (bf16[1024,1,896]{0,2,1:T(8,128)(2,1)S(1)}, bf16[1024,1,896]{0,2,1:T(8,128)(2,1)}, u32[]{:S(2)}) copy-start(bf16[1024,1,896]{0,2,1:T(8,128)(2,1)} %copy.86) | copy-start | bytes 5505028
Sparse Core Ops, SparseCore 0:
  10.1 320.8 all-gather.1
where the time goes:
time: 547 us; the launch traced here: 545 us
  blocking collectives  213 us (39%)
  local copies, waits for them, and re-layouts  120 us (22%)
  waiting for transfers between devices  110 us (20%)
  matrix products  52.6 us (10%)
  other arithmetic  19.5 us (4%)
  starting transfers between devices  15.3 us (3%)
  between operations  14.3 us (3%)
    psum x1, blocking collectives, local(): lax.psum(down_term(row_part, row_slots, down_cols, active_slots), 'col')  199 us
    all_gather x1, waiting for transfers between devices, local(): weight_piece = lax.all_gather(projection_weight, 'col', axis=0, tiled=True)  66 us
    all_gather x1, local copies, waits for them, and re-layouts, local(): weight_piece = lax.all_gather(projection_weight, 'col', axis=0, tiled=True)  51.4 us
    ppermute x1, waiting for transfers between devices, shifted(): return lax.ppermute(block, axis, route)  41.3 us
    dot_general x1, matrix products, local(): jnp.dot(own_rows, flat_piece, preferred_element_type=jnp.float32)  28.4 us
    gather x1, local copies, waits for them, and re-layouts, local(): jnp.take(page_window, pick_rows, axis=0)  16.6 us
    concatenate x2, local copies, waits for them, and re-layouts, local(): jnp.concatenate([prev_kv, own_kv, jnp.zeros((PAGE, 2, head_column_span),...  15.3 us
    all_gather x1, blocking collectives, local(): lax.all_gather(summed.astype(jnp.bfloat16), 'row', axis=0, tiled=True)  13.7 us
  transfers between devices with their start and end apart: 4, of which 3 were waited for; matrix products, arithmetic and copies ran while one was open for 16% of the time, Pallas kernels for 0%

commit v1 on v0

--- a/solution.py
+++ b/solution.py
@@ -9,6 +9,19 @@
 SLOTS_DEV = 10
 adapter_scale = 2.0
 masked_score = -1e30
+
+
+def _supply_all_windows(t0, net_axis="col"):
+    u_next = jnp.concatenate(
+        lax.all_to_all(
+            jnp.stack([t0 for _ in range(lax.axis_size(net_axis))], axis=0),
+            axis_name=net_axis,
+            split_axis=0,
+            concat_axis=0,
+        ),
+        0,
+    )
+    return u_next
 
 
 def shifted(block, axis, distance):
@@ -79,7 +92,7 @@
     )
     down_cols = down_weight_slices.reshape(width_loc, -1)
     own_rows = lax.all_to_all(normed, "col", split_axis=0, concat_axis=1, tiled=True)
-    weight_piece = lax.all_gather(projection_weight, "col", axis=0, tiled=True)
+    weight_piece = _supply_all_windows(projection_weight)
     flat_piece = weight_piece.reshape(weight_piece.shape[0], -1)
     projection_total = jnp.dot(own_rows, flat_piece, preferred_element_type=jnp.float32)
     rows_per = tok_all // row_count

time: 547 us -> 1220 us (2.23)
  waiting for transfers between devices: 110 us -> 734 us
  local copies, waits for them, and re-layouts: 120 us -> 210 us
  blocking collectives: 213 us -> 169 us
  between operations: 14.3 us -> 0.91 us
  starting transfers between devices: 15.3 us -> 28.3 us
    all_to_all x1, waiting for transfers between devices: 1.74 us -> 695 us  [_supply_all_windows(): lax.all_to_all(jnp.stack([t0 for _ in range(lax.axis_size(net_axis))], ax...]
    another operation x1 -> x3, local copies, waits for them, and re-layouts: 0.1 us -> 83.9 us  [the longest x1 69.9 us: local(): flat_piece = weight_piece.reshape(weight_piece.shape[0], -1)]
    all_gather x1 -> x0, waiting for transfers between devices: 66 us -> none  [local(): weight_piece = lax.all_gather(projection_weight, 'col', axis=0, tiled=True)]
    psum x1, blocking collectives: 199 us -> 138 us  [local(): lax.psum(down_term(row_part, row_slots, down_cols, active_slots), 'col')]
    all_to_all x0 -> x1, local copies, waits for them, and re-layouts: none -> 59.7 us  [_supply_all_windows(): lax.all_to_all(jnp.stack([t0 for _ in range(lax.axis_size(net_axis))], ax...]
    all_gather x1 -> x0, local copies, waits for them, and re-layouts: 51.4 us -> none  [local(): weight_piece = lax.all_gather(projection_weight, 'col', axis=0, tiled=True)]
    all_to_all x0 -> x1, blocking collectives: none -> 16 us  [local(): lax.all_to_all(adapter_down_weight, 'col', split_axis=0, concat_axis=1, t...]
    all_to_all x1, starting transfers between devices: 5.93 us -> 18.4 us  [local(): lax.all_to_all(normed, 'col', split_axis=0, concat_axis=1, tiled=True)]
  transfers between devices with their start and end apart: 4 -> 3, of which waited for: 3 -> 2; matrix products, arithmetic and copies ran while one was open for 16% -> 13% of each run, Pallas kernels for 0% -> 0%
where the time goes in v1:
time: 1220 us; the launch traced here: 1210 us
  waiting for transfers between devices  734 us (60%)
  local copies, waits for them, and re-layouts  210 us (17%)
  blocking collectives  169 us (14%)
  matrix products  52.6 us (4%)
  starting transfers between devices  28.3 us (2%)
  other arithmetic  19.5 us (2%)
    all_to_all x1, waiting for transfers between devices, _supply_all_windows(): lax.all_to_all(jnp.stack([t0 for _ in range(lax.axis_size(net_axis))], ax...  695 us
    psum x1, blocking collectives, local(): lax.psum(down_term(row_part, row_slots, down_cols, active_slots), 'col')  138 us
    another operation x1, local copies, waits for them, and re-layouts, local(): flat_piece = weight_piece.reshape(weight_piece.shape[0], -1)  69.9 us
    all_to_all x1, local copies, waits for them, and re-layouts, _supply_all_windows(): lax.all_to_all(jnp.stack([t0 for _ in range(lax.axis_size(net_axis))], ax...  59.7 us
    ppermute x1, waiting for transfers between devices, shifted(): return lax.ppermute(block, axis, route)  38.9 us
    dot_general x1, matrix products, local(): jnp.dot(own_rows, flat_piece, preferred_element_type=jnp.float32)  28.4 us
  transfers between devices with their start and end apart: 3, of which 2 were waited for; matrix products, arithmetic and copies ran while one was open for 13% of the time, Pallas kernels for 0%

profile of v1, /device:TPU:6, one launch (start us, length us, event | category | flops | bytes accessed | tf_op | source)
XLA Modules:
  0.0 1214.2 jit_solution(4682268852704500293)
XLA Ops:
  0.6 0.5 broadcast.229
  1.1 1.9 reduce.3
  3.1 0.9 copy.106
  4.0 1.7 reshape.317
  5.8 16.0 %all_to_all.39 = bf16[16,2,7168]{2,1,0:T(2,128)(2,1)S(1)} all-to-all(bf16[16,2,7168]{2,1,0:T(2,128)(2,1)S(1)} %reshape.317), channel_id=1, replica_groups=mesh['row'=8,'col'=16] {'col'}, dimensions={0} | all-to-all | bytes 917504 | tf_op jit(solution)/shard_map/all_to_all | solution.py:90
  21.8 13.8 %stack.8 = bf16[16,448,3,896]{3,1,2,0:T(8,128)(2,1)} broadcast(bf16[448,3,896]{2,0,1:T(8,128)(2,1)} %param.9), dimensions={1,2,3} | broadcast | bytes 40943616 | tf_op jit(solution)/shard_map/stack | solution.py:17
  35.6 8.0 all-to-all-start.1
  43.6 6.9 copy.105
  50.5 695.3 %all-to-all-done.1 = bf16[16,448,3,896]{3,1,2,0:T(8,128)(2,1)} async-done(((bf16[16,448,3,896]{3,1,2,0:T(8,128)(2,1)}), bf16[16,448,3,896]{3,1,2,0:T(8,128)(2,1)}, u32[]{:S(2)}, u32[]{:S(2)}) %all-to-all-start.1) | async-done | bytes 38535200 | tf_op jit(solution)/shard_map/all_to_all | solution.py:16
  745.8 18.4 %all-to-all-start = ((bf16[16,512,448]{1,2,0:T(8,128)(2,1)}), bf16[16,512,448]{1,2,0:T(8,128)(2,1)}, u32[]{:S(2)}, u32[]{:S(2)}) async-start(bf16[16,512,448]{1,2,0:T(8,128)(2,1)} %bitcast.61), calls=%async_computation | async-start | bytes 14680064 | tf_op jit(solution)/shard_map/all_to_all | solution.py:94
  764.2 0.0 copy-done.4
  764.2 0.1 copy.83
  764.3 0.1 reduce-window.9
  764.4 0.1 reduce
  764.5 0.0 copy-done.6
  764.5 0.0 copy-done.7
  764.5 0.1 select_reduce_fusion.4
  764.6 0.1 convert_reduce_fusion.2
  764.7 0.1 select_reduce_fusion.3
  764.8 0.1 convert_reduce_fusion
  765.0 0.1 select_reduce_fusion.2
  765.1 0.1 fusion.21
  765.2 0.1 subtract_clamp_fusion
  765.3 0.0 copy-done.1
  765.3 0.1 fusion.36
  765.4 4.2 reshape.318
  769.6 7.0 copy.85
  776.6 0.6 all_to_all.34
  777.3 1.9 select_reduce_fusion.1
  779.2 138.0 %all-reduce.1 = bf16[1024,32]{0,1:T(8,128)(2,1)S(1)} all-reduce(f32[1024,32]{0,1:T(8,128)S(1)} %select_reduce_fusion.1), channel_id=1, replica_groups=mesh['row'=8,'col'=16] {'col'}, use_global_device_ids=true, to_apply=%region_7.8 | all-reduce | flops 32768 | bytes 196608 | tf_op jit(solution)/shard_map/psum | solution.py:103
  917.2 14.5 %all_gather.3 = bf16[8192,32]{0,1:T(8,128)(2,1)S(1)} all-gather(bf16[1024,32]{0,1:T(8,128)(2,1)S(1)} %all-reduce.1), channel_id=1, replica_groups=mesh['row'=8,'col'=16] {'row'}, dimensions={0}, use_global_device_ids=true | all-gather | bytes 589824 | tf_op jit(solution)/shard_map/all_gather | solution.py:104
  931.8 59.7 %copy.82 = bf16[16,448,3,896]{1,0,3,2:T(8,128)(2,1)} copy(bf16[16,448,3,896]{3,1,2,0:T(8,128)(2,1)} %all-to-all-done.1) | data formatting | bytes 77070336 | tf_op jit(solution)/shard_map/all_to_all | solution.py:16
  991.5 69.9 %reshape_reshape.3 = bf16[7168,2688]{0,1:T(8,128)(2,1)} reshape(bf16[16,448,3,896]{1,0,3,2:T(8,128)(2,1)} %copy.82) | data formatting | bytes 77070336 | tf_op jit(solution)/shard_map/reshape;reshape | solution.py:96
  1061.4 0.0 all-to-all-done
  1061.4 28.4 %fusion.38 = f32[512,2688]{1,0:T(8,128)} fusion(bf16[512,7168]{0,1:T(8,128)(2,1)} %bitcast.1, bf16[7168,2688]{0,1:T(8,128)(2,1)} %reshape_reshape.3), kind=kOutput, calls=%fused_computation.78 | convolution fusion | flops 19730006016 | bytes 51380224 | tf_op jit(solution)/shard_map/dot_general | solution.py:97
  1089.8 1.6 fusion.16
  1091.4 2.0 fusion.15
  1093.4 1.4 pad_maximum_fusion
  1094.8 1.9 collective-permute-start
  1096.8 0.1 add.145
  1096.9 0.0 copy-done.5
  1096.9 0.1 copy.92
  1097.0 0.1 eq.123
  1097.1 0.1 min.20
  1097.2 0.2 fusion.24
  1097.4 0.1 fusion.25
  1097.5 0.1 fusion.28
  1097.6 0.1 iota_compare_fusion.4
  1097.7 1.3 compare_and_fusion
  1099.0 2.0 fusion.10
  1100.9 1.5 copy.88
  1102.5 38.9 %collective-permute-done = bf16[512,2,896]{2,0,1:T(8,128)(2,1)} collective-permute-done((bf16[512,2,896]{2,0,1:T(8,128)(2,1)}, bf16[512,2,896]{2,0,1:T(8,128)(2,1)}, u32[]{:S(2)}, u32[]{:S(2)}) %collective-permute-start) | collective-permute-done | bytes 1835040 | tf_op jit(solution)/shard_map/ppermute | solution.py:30
  1141.4 3.1 maximum_maximum_fusion
  1144.6 15.3 %copy.93 = bf16[1152,2,896]{2,1,0:T(2,128)(2,1)} copy(bf16[1152,2,896]{2,0,1:T(8,128)(2,1)S(1)} %maximum_maximum_fusion) | data formatting | bytes 8257536 | tf_op jit(solution)/shard_map/concatenate | solution.py:158
  1159.8 1.8 maximum_maximum_fusion.1
  1161.6 1.5 fusion.35
  1163.2 3.9 copy.89
  1167.1 2.4 copy.87
  1169.5 0.0 copy-done.2
  1169.5 12.7 %fusion.37 = (f32[7,512]{1,0:T(8,128)S(1)}, bf16[7,512,1024]{2,1,0:T(8,128)(2,1)}) fusion(pred[512,1024]{1,0:T(8,128)(4,1)S(1)} %copy-done.3, bf16[512,7,128]{0,2,1:T(8,128)(2,1)S(1)} %bitcast.70, bf16[1024,7,128]{0,2,1:T(8,128)(2,1)} %bitcast.64), kind=kOutput, calls=%fused_computation.77 | convolution fusion | flops 1904739328 | bytes 10631168 | tf_op jit(solution)/shard_map/sub | solution.py:147
  1182.2 5.7 fusion.12
  1187.8 1.3 copy.94
  1189.1 16.6 %gather_fusion = bf16[1280,2,896]{2,1,0:T(2,128)(2,1)} fusion(bf16[1152,2,896]{2,1,0:T(2,128)(2,1)} %copy.93, s32[2048]{0:T(1024)S(1)} %pad_clamp_fusion), kind=kCustom, calls=%fused_computation | custom fusion | bytes 9180160 | tf_op jit(solution)/shard_map/jit(_take)/gather | solution.py:174
  1205.7 8.5 broadcast_select_fusion.1
  (26 shorter events, 0.2 us)
Async XLA Ops:
  35.6 710.2 %all-to-all-start.1 = ((bf16[16,448,3,896]{3,1,2,0:T(8,128)(2,1)}), bf16[16,448,3,896]{3,1,2,0:T(8,128)(2,1)}, u32[]{:S(2)}, u32[]{:S(2)}) async-start(bf16[16,448,3,896]{3,1,2,0:T(8,128)(2,1)} %stack.8), calls=%async_computation.1 | async-start | bytes 77070336 | tf_op jit(solution)/shard_map/all_to_all | solution.py:16
  745.8 18.4 %copy-start.4 = (s32[64]{0:T(128)S(1)}, s32[64]{0:T(128)}, u32[]{:S(2)}) copy-start(s32[64]{0:T(128)} %param.12) | copy-start | bytes 772
  745.8 18.7 %copy-start.6 = (s32[64]{0:T(128)S(1)}, s32[64]{0:T(128)}, u32[]{:S(2)}) copy-start(s32[64]{0:T(128)} %param.13) | copy-start | bytes 772
  745.8 18.7 %copy-start.7 = (s32[16]{0:T(128)S(1)}, s32[16]{0:T(128)}, u32[]{:S(2)}) copy-start(s32[16]{0:T(128)} %param.14) | copy-start | bytes 196
  745.8 19.5 %copy-start.1 = (bf16[16,2,16,896]{3,2,1,0:T(8,128)(2,1)S(1)}, bf16[16,2,16,896]{3,2,1,0:T(8,128)(2,1)}, u32[]{:S(2)}) copy-start(bf16[16,2,16,896]{3,2,1,0:T(8,128)(2,1)} %param.11) | copy-start | bytes 2752516
  745.8 315.6 %all-to-all-start = ((bf16[16,512,448]{1,2,0:T(8,128)(2,1)}), bf16[16,512,448]{1,2,0:T(8,128)(2,1)}, u32[]{:S(2)}, u32[]{:S(2)}) async-start(bf16[16,512,448]{1,2,0:T(8,128)(2,1)} %bitcast.61), calls=%async_computation | async-start | bytes 14680064 | tf_op jit(solution)/shard_map/all_to_all | solution.py:94
  1089.8 7.0 copy-start.5
  1094.8 46.6 %collective-permute-start = (bf16[512,2,896]{2,0,1:T(8,128)(2,1)}, bf16[512,2,896]{2,0,1:T(8,128)(2,1)}, u32[]{:S(2)}, u32[]{:S(2)}) collective-permute-start(bf16[512,2,896]{2,0,1:T(8,128)(2,1)} %pad_maximum_fusion), channel_id=1, source_target_pairs={{0,1},{1,2},{2,3},{3,4},{4,5},{5,6},{6,7},{7,8},{8,9},{9,10},{10,1... | collective-permute-start | bytes 5505032 | tf_op jit(solution)/shard_map/ppermute | solution.py:30
  1163.2 6.3 copy-start.2
  1163.2 6.3 copy-start.3
  1169.5 12.7 %copy-start = (bf16[1024,1,896]{0,2,1:T(8,128)(2,1)S(1)}, bf16[1024,1,896]{0,2,1:T(8,128)(2,1)}, u32[]{:S(2)}) copy-start(bf16[1024,1,896]{0,2,1:T(8,128)(2,1)} %copy.87) | copy-start | bytes 5505028
